TPU v7x, 32 devices: a whole 2x2x4 slice. The times are simulated.
32 devices in a mesh: fsdp: 8 (over z, x), head: 2 (over core), tensor: 2 (over y).
Axes of the slice: x: 2, y: 2, z: 4, core: 2. Of those that a mesh axis runs over, the one named last changes fastest.
Arguments:
- block_in: bfloat16 [4096, 1024], P('fsdp'), may hold values from -6 to 6
- cotangent: bfloat16 [4096, 1024], P('fsdp'), may hold values from -6 to 6
- norm_gain: float32 [1024], replicated, may hold values from 0.5 to 1.5
- w_x: bfloat16 [1024, 32, 64], P('fsdp', 'head', 'tensor'), may hold values from -0.1875 to 0.1875
- w_z: bfloat16 [1024, 32, 64], P('fsdp', 'head', 'tensor'), may hold values from -0.1875 to 0.1875
- w_bc: bfloat16 [1024, 2, 128], P('fsdp'), may hold values from -0.1875 to 0.1875
- w_dt: bfloat16 [1024, 32], P('fsdp', 'head'), may hold values from -0.1875 to 0.1875
- conv_x: float32 [32, 64, 4], P('head', 'tensor'), may hold values from -3 to 3
- conv_bc: float32 [2, 128, 4], replicated, may hold values from -3 to 3
- dt_bias: float32 [32], P('head'), may hold values from -6 to -2
- a_log: float32 [32], P('head'), may hold values from -1.5 to 0.5
- skip: float32 [32], P('head'), may hold values from 0.5 to 1.5
- gate_gain: float32 [32, 64], P('head', 'tensor'), may hold values from 0.5 to 1.5
- w_out: bfloat16 [32, 64, 1024], P('head', 'tensor', 'fsdp'), may hold values from -0.125 to 0.125
Outputs:
- block_out: bfloat16 [4096, 1024], P('fsdp')
- grad_in: float32 [4096, 1024], P('fsdp')
- grad_norm_gain: float32 [1024], replicated
- grad_w_x: float32 [1024, 32, 64], P('fsdp', 'head', 'tensor')
- grad_w_z: float32 [1024, 32, 64], P('fsdp', 'head', 'tensor')
- grad_w_bc: float32 [1024, 2, 128], P('fsdp')
- grad_w_dt: float32 [1024, 32], P('fsdp', 'head')
- grad_conv_x: float32 [32, 64, 4], P('head', 'tensor')
- grad_conv_bc: float32 [2, 128, 4], replicated
- grad_dt_bias: float32 [32], P('head')
- grad_a_log: float32 [32], P('head')
- grad_skip: float32 [32], P('head')
- grad_gate_gain: float32 [32, 64], P('head', 'tensor')
- grad_w_out: float32 [32, 64, 1024], P('head', 'tensor', 'fsdp')
All inputs are finite; a program needn't handle non-finite values.
Results may differ from a plain program's by a relative error of at most 0.011.
Values may be sent and summed in bfloat16 or wider, within the bound.
A program may use at most 128 MiB of HBM per device.

v0:
```python
from functools import partial
import jax
import jax.numpy as jnp
from jax import lax
from jax.sharding import PartitionSpec as P

SPAN = 256
EPSILON = 1e-05
PRECISE = lax.Precision.HIGHEST


def causal_conv(signal, kernel):
    taps = kernel.shape[1]
    length = signal.shape[0]
    padded = jnp.pad(signal, ((taps - 1, 0), (0, 0)))
    total = jnp.zeros_like(signal)
    for offset in range(taps):
        total = total + padded[offset : offset + length] * kernel[:, offset]
    return total


def conv_silu(signal, kernel):
    return jax.nn.silu(causal_conv(signal, kernel))


def silu_slope(value):
    sigma = jax.nn.sigmoid(value)
    return sigma * (1.0 + value * (1.0 - sigma))


def scan_spans(values, step_size, rate, b_maps, c_maps, block):
    length, head_count, channels = values.shape
    blocks = length // block
    logs = (step_size * rate).reshape(blocks, block, head_count)
    cums = jnp.cumsum(logs, axis=1)
    x_blocks = values.reshape(blocks, block, head_count, channels)
    dt_blocks = step_size.reshape(blocks, block, head_count)
    b_blocks = b_maps.reshape(blocks, block, -1)
    c_blocks = c_maps.reshape(blocks, block, -1)
    scores = jnp.einsum("cln,csn->cls", c_blocks, b_blocks, precision=PRECISE)
    causal = (jnp.arange(block)[:, None] >= jnp.arange(block)[None, :])[None, :, :, None]
    gaps = cums[:, :, None, :] - cums[:, None, :, :]
    decays = jnp.where(causal, jnp.exp(jnp.where(causal, gaps, 0.0)), 0.0)
    mixing = scores[..., None] * decays * dt_blocks[:, None, :, :]
    intra_part = jnp.einsum("clsh,cshp->clhp", mixing, x_blocks, precision=PRECISE)
    to_end = jnp.exp(cums[:, -1:, :] - cums) * dt_blocks
    states = jnp.einsum("csh,csn,cshp->chpn", to_end, b_blocks, x_blocks, precision=PRECISE)
    whole_decay = jnp.exp(cums[:, -1, :])
    carried = []
    running = jnp.zeros_like(states[0])
    for position in range(blocks):
        carried.append(running)
        running = running * whole_decay[position][:, None, None] + states[position]
    entering = jnp.stack(carried)
    inter_part = jnp.einsum(
        "cln,clh,chpn->clhp", c_blocks, jnp.exp(cums), entering, precision=PRECISE
    )
    return (intra_part + inter_part).reshape(length, head_count, channels)


def mixer(values, dt_raw, dt_bias, a_log, skip, b_maps, c_maps, block):
    step_size = jax.nn.softplus(dt_raw + dt_bias)
    rate = -jnp.exp(a_log)
    return scan_spans(values, step_size, rate, b_maps, c_maps, block) + skip[:, None] * values


def on_device(
    block_in,
    cotangent,
    norm_gain,
    w_x,
    w_z,
    w_bc,
    w_dt,
    conv_x,
    conv_bc,
    dt_bias,
    a_log,
    skip,
    gate_gain,
    w_out,
):
    length, model_width = block_in.shape
    head_count, head_width, taps = conv_x.shape
    state_size = conv_bc.shape[1]
    inner_width = head_count * head_width
    group_count = lax.axis_size("head") * lax.axis_size("tensor")
    full_inner = inner_width * group_count
    weights = (w_x, w_z, w_bc, w_dt, w_out)
    gathered = (
        lax.all_gather(weights[0], "fsdp", axis=0, tiled=True),
        lax.all_gather(weights[1], "fsdp", axis=0, tiled=True),
        lax.all_gather(weights[2], "fsdp", axis=0, tiled=True),
        lax.all_gather(weights[3], "fsdp", axis=0, tiled=True),
        lax.all_gather(weights[4], "fsdp", axis=2, tiled=True),
    )
    weight_x = gathered[0].reshape(model_width, inner_width)
    weight_z = gathered[1].reshape(model_width, inner_width)
    weight_bc = gathered[2].reshape(model_width, 2 * state_size)
    weight_dt = gathered[3]
    weight_out = gathered[4].reshape(inner_width, model_width)
    kernel_x = conv_x.reshape(inner_width, taps)
    kernel_bc = conv_bc.reshape(2 * state_size, taps)
    gain_flat = gate_gain.reshape(inner_width)
    features = block_in.astype(jnp.float32)
    scale_in = lax.rsqrt(jnp.mean(features * features, axis=1, keepdims=True) + EPSILON)
    normed = (features * scale_in * norm_gain).astype(jnp.bfloat16)
    x_raw = jnp.dot(normed, weight_x, preferred_element_type=jnp.float32)
    z_raw = jnp.dot(normed, weight_z, preferred_element_type=jnp.float32)
    bc_raw = jnp.dot(normed, weight_bc, preferred_element_type=jnp.float32)
    dt_raw = jnp.dot(normed, weight_dt, preferred_element_type=jnp.float32)
    x_act = conv_silu(x_raw, kernel_x).astype(jnp.bfloat16)
    bc_act = conv_silu(bc_raw, kernel_bc).astype(jnp.bfloat16)
    values = x_act.astype(jnp.float32).reshape(length, head_count, head_width)
    b_maps = bc_act[:, :state_size].astype(jnp.float32)
    c_maps = bc_act[:, state_size:].astype(jnp.float32)
    mixed = mixer(values, dt_raw, dt_bias, a_log, skip, b_maps, c_maps, SPAN).reshape(
        length, inner_width
    )
    gated = mixed * jax.nn.silu(z_raw)
    square_sum = lax.psum(jnp.sum(gated * gated, axis=1), ("head", "tensor"))
    scale_out = lax.rsqrt(square_sum / full_inner + EPSILON)[:, None]
    normed_out = (gated * scale_out * gain_flat).astype(jnp.bfloat16)
    partial_out = jnp.dot(normed_out, weight_out, preferred_element_type=jnp.float32)
    summed = lax.psum(partial_out, ("head", "tensor"))
    block_out = (summed + features).astype(jnp.bfloat16)
    again = (
        lax.all_gather(weights[0], "fsdp", axis=0, tiled=True),
        lax.all_gather(weights[1], "fsdp", axis=0, tiled=True),
        lax.all_gather(weights[2], "fsdp", axis=0, tiled=True),
        lax.all_gather(weights[3], "fsdp", axis=0, tiled=True),
        lax.all_gather(weights[4], "fsdp", axis=2, tiled=True),
    )
    back_x = again[0].reshape(model_width, inner_width)
    back_z = again[1].reshape(model_width, inner_width)
    back_bc = again[2].reshape(model_width, 2 * state_size)
    back_dt = again[3]
    back_out = again[4].reshape(inner_width, model_width)
    upstream = cotangent.astype(jnp.float32)
    d_normed_out = jnp.dot(cotangent, back_out.T, preferred_element_type=jnp.float32)
    g_w_out = jnp.dot(normed_out.T, cotangent, preferred_element_type=jnp.float32)
    g_gate_gain = jnp.sum(d_normed_out * gated * scale_out, axis=0)
    d_hat = d_normed_out * gain_flat
    inner_sum = lax.psum(jnp.sum(d_hat * gated, axis=1), ("head", "tensor"))[:, None]
    d_gated = scale_out * d_hat - gated * scale_out**3 * inner_sum / full_inner
    d_mixed = d_gated * jax.nn.silu(z_raw)
    d_z = (d_gated * mixed * silu_slope(z_raw)).astype(jnp.bfloat16)
    _, pullback = jax.vjp(
        partial(mixer, block=SPAN), values, dt_raw, dt_bias, a_log, skip, b_maps, c_maps
    )
    d_xs, d_dt, g_dt_bias, g_a_log, g_skip, d_b, d_c = pullback(
        d_mixed.reshape(length, head_count, head_width)
    )
    d_dt, g_dt_bias, g_a_log, g_skip = lax.psum((d_dt, g_dt_bias, g_a_log, g_skip), "tensor")
    d_bc = lax.psum(jnp.concatenate([d_b, d_c], axis=1), ("head", "tensor"))
    _, pull_x = jax.vjp(conv_silu, x_raw, kernel_x)
    d_x_raw, g_conv_x = pull_x(d_xs.reshape(length, inner_width))
    _, pull_bc = jax.vjp(conv_silu, bc_raw, kernel_bc)
    d_bc_raw, g_conv_bc = pull_bc(d_bc)
    d_x_b = d_x_raw.astype(jnp.bfloat16)
    d_bc_b = d_bc_raw.astype(jnp.bfloat16)
    d_dt_b = d_dt.astype(jnp.bfloat16)
    g_w_x = jnp.dot(normed.T, d_x_b, preferred_element_type=jnp.float32)
    g_w_z = jnp.dot(normed.T, d_z, preferred_element_type=jnp.float32)
    g_w_bc = jnp.dot(normed.T, d_bc_b, preferred_element_type=jnp.float32)
    g_w_dt = jnp.dot(normed.T, d_dt_b, preferred_element_type=jnp.float32)
    local_part = (
        jnp.dot(d_x_b, back_x.T, preferred_element_type=jnp.float32)
        + jnp.dot(d_z, back_z.T, preferred_element_type=jnp.float32)
        + jnp.dot(d_dt_b, back_dt.T, preferred_element_type=jnp.float32)
        * (1.0 / lax.axis_size("tensor"))
    )
    d_normed = lax.psum(local_part, ("head", "tensor")) + jnp.dot(
        d_bc_b, back_bc.T, preferred_element_type=jnp.float32
    )
    g_norm_gain = jnp.sum(d_normed * features * scale_in, axis=0)
    d_in_hat = d_normed * norm_gain
    grad_in = (
        scale_in * d_in_hat
        - features * scale_in**3 * jnp.mean(d_in_hat * features, axis=1, keepdims=True)
        + upstream
    )
    big_grads = (
        lax.psum_scatter(
            g_w_x.reshape(model_width, head_count, head_width),
            "fsdp",
            scatter_dimension=0,
            tiled=True,
        ),
        lax.psum_scatter(
            g_w_z.reshape(model_width, head_count, head_width),
            "fsdp",
            scatter_dimension=0,
            tiled=True,
        ),
        lax.psum_scatter(g_w_bc, "fsdp", scatter_dimension=0, tiled=True),
        lax.psum_scatter(g_w_dt, "fsdp", scatter_dimension=0, tiled=True),
        lax.psum_scatter(
            g_w_out.reshape(head_count, head_width, model_width),
            "fsdp",
            scatter_dimension=2,
            tiled=True,
        ),
    )
    owned_bc = big_grads[2].reshape(-1, 2, state_size)
    small = lax.psum(
        (
            g_norm_gain,
            g_conv_x.reshape(head_count, head_width, taps),
            g_conv_bc.reshape(2, state_size, taps),
            g_dt_bias,
            g_a_log,
            g_skip,
            g_gate_gain.reshape(head_count, head_width),
        ),
        "fsdp",
    )
    return (
        block_out,
        grad_in,
        small[0],
        big_grads[0],
        big_grads[1],
        owned_bc,
        big_grads[3],
        small[1],
        small[2],
        small[3],
        small[4],
        small[5],
        small[6],
        big_grads[4],
    )


def solution(mesh):
    return jax.shard_map(
        on_device,
        mesh=mesh,
        in_specs=(
            P("fsdp", None),
            P("fsdp", None),
            P(),
            P("fsdp", "head", "tensor"),
            P("fsdp", "head", "tensor"),
            P("fsdp", None, None),
            P("fsdp", "head"),
            P("head", "tensor", None),
            P(),
            P("head"),
            P("head"),
            P("head"),
            P("head", "tensor"),
            P("head", "tensor", "fsdp"),
        ),
        out_specs=(
            P("fsdp", None),
            P("fsdp", None),
            P(),
            P("fsdp", "head", "tensor"),
            P("fsdp", "head", "tensor"),
            P("fsdp", None, None),
            P("fsdp", "head"),
            P("head", "tensor", None),
            P(),
            P("head"),
            P("head"),
            P("head"),
            P("head", "tensor"),
            P("head", "tensor", "fsdp"),
        ),
        check_vma=False,
    )
```

profile of v0, /device:TPU:0, one launch (start us, length us, event | category | flops | bytes accessed | tf_op | source)
XLA Modules:
  0.0 668.9 jit_solution(9409954152697508148)
XLA Ops:
  13.0 28.3 %all_gather.22 = bf16[1024,16]{0,1:T(8,128)(2,1)S(1)} all-gather(bf16[128,16]{0,1:T(8,128)(2,1)} %param.20), channel_id=1, replica_groups=mesh['fsdp'=8,'head'=2,'tensor'=2] {'fsdp'}, dimensions={0}, use_global_device_ids=true | all-gather | bytes 36864 | tf_op jit(solution)/shard_map/all_gather | solution.py:94
  41.3 2.3 broadcast_multiply_fusion.8
  48.1 32.0 %all_gather.21 = bf16[1024,2,128]{2,1,0:T(2,128)(2,1)S(1)} all-gather(bf16[128,2,128]{2,1,0:T(2,128)(2,1)S(1)} %copy-done.27), channel_id=1, replica_groups=mesh['fsdp'=8,'head'=2,'tensor'=2] {'fsdp'}, dimensions={0}, use_global_device_ids=true | all-gather | bytes 589824 | tf_op jit(solution)/shard_map/all_gather | solution.py:93
  90.0 6.3 fusion.38
  98.5 3.5 multiply_reduce_fusion.9
  102.1 7.9 %psum.112 = f32[512]{0:T(512)S(1)} all-reduce(f32[512]{0:T(512)S(1)} %get-tuple-element.106), channel_id=1, replica_groups=mesh['fsdp'=8,'head'=2,'tensor'=2] {'head','tensor'}, use_global_device_ids=true, to_apply=%region_4.5 | all-reduce | flops 512 | bytes 4096 | tf_op jit(solution)/shard_map/psum | solution.py:121
  110.0 25.5 %all-gather.8.cloned.1.call-done = bf16[16,32,1024]{2,1,0:T(8,128)(2,1)} async-done(((bf16[16,32,128]{2,1,0:T(8,128)(2,1)}), bf16[16,32,1024]{2,1,0:T(8,128)(2,1)}) %all-gather.8.cloned.1.call-update) | async-done | bytes 1048592 | tf_op jit(solution)/shard_map/all_gather | solution.py:95
  135.5 3.9 multiply_reduce_fusion.3
  139.4 7.5 %psum.114 = f32[512]{0:T(512)S(1)} all-reduce(f32[512]{0:T(512)S(1)} %get-tuple-element.77), channel_id=1, replica_groups=mesh['fsdp'=8,'head'=2,'tensor'=2] {'head','tensor'}, use_global_device_ids=true, to_apply=%region_7.8 | all-reduce | flops 512 | bytes 4096 | tf_op jit(solution)/shard_map/psum | solution.py:144
  146.9 4.2 fusion.45
  152.5 2.9 reshape_reshape.8
  157.3 2.6 convolution_bitcast_fusion.1
  160.8 2.6 convolution_bitcast_fusion.2
  164.0 11.4 %fusion.9 = (f32[2,256,16]{1,2,0:T(8,128)}, f32[2,256,16]{1,2,0:T(8,128)}, f32[2,256,16]{1,2,0:T(8,128)}, f32[2,256,256]{2,1,0:T(8,128)}) fusion(f32[2,256,16]{1,2,0:T(8,128)S(1)} %bitcast.241, f32[2,256,16]{1,2,0:T(8,128)S(1)} %copy-done.26, f32[2,256,256]{2,1,0:T(8,128)S(1)} %copy-done.20, pred[256,256]{1,0:T(8,128)(4,1)S(1)} %copy-done.29, ...), kind=kOutput, calls=%fused_computation.18 | convolution fusion | flops 836608000 | bytes 2850816 | tf_op jit(solution)/shard_map/transpose(jvp(clsh,cshp->clhp))/dot_general | solution.py:45
  175.5 8.0 %fusion.41 = f32[2,256,16,32]{1,3,2,0:T(8,128)} fusion(f32[2,256,16]{1,2,0:T(8,128)S(1)} %bitcast.242, f32[2,256,16]{1,2,0:T(8,128)S(1)} %copy-done.26, f32[2,256,256]{2,1,0:T(8,128)S(1)} %copy-done.20, pred[256,256]{1,0:T(8,128)(4,1)S(1)} %copy-done.29, f32[2,256,16,32]{1,3,2,0:T(8,128)S(1)} %fusion.58, f32[2,16,32,256]{3,0,2,1:T(2,128)S(1)} %bitcast.207, ...), kind=kOutput, calls=%fused_computation.48 | convolution fusion | flops 816316416 | bytes 3833856 | tf_op jit(solution)/shard_map/transpose(jvp(clsh,cshp->clhp))/dot_general | solution.py:45
  190.2 2.5 convolution_add_fusion.2
  196.9 2.6 copy.141
  199.9 5.0 reduce-window.16
  205.3 3.6 fusion.118
  214.6 8.2 %all-reduce.25 = (bf16[512,16]{0,1:T(8,128)(2,1)S(1)}, f32[16]{0:T(128)S(1)}, f32[16]{0:T(128)S(1)}, f32[16]{0:T(128)S(1)}) all-reduce(f32[512,16]{0,1:T(8,128)S(1)} %get-tuple-element.105, f32[16]{0:T(128)S(1)} %get-tuple-element.104, f32[16]{0:T(128)S(1)} %negate_multiply_fusion, ...), channel_id=1, replica_groups=mesh['fsdp'=8,'head'=2,'tensor'=2] {'tensor'}, use_global_device_ids=true, to_apply=%region_15.16 | all-reduce | flops 8240 | bytes 49536 | tf_op jit(solution)/shard_map/psum | solution.py:154
  222.8 4.0 multiply_add_fusion
  227.0 92.6 %all-reduce.28.cloned.1.call-done = (f32[512,1024]{1,0:T(8,128)}, f32[512,1024]{1,0:T(8,128)}, f32[512,256]{1,0:T(8,128)}) async-done(((f32[512,1024]{1,0:T(8,128)}, f32[512,1024]{1,0:T(8,128)}, f32[512,256]{1,0:T(8,128)}), (f32[512,1024]{1,0:T(8,128)}, f32[512,1024]{1,0:T(8,128)}, f32[512,256]{1,0:T(8,128)})) %all-reduce.28.cloned.1.call-update) | async-done | bytes 4718608 | tf_op jit(solution)/shard_map/psum | solution.py:125
  324.7 3.4 fusion.92
  329.1 2.2 fusion.97
  333.8 2.6 fusion.31
  336.5 38.1 %all-reduce.23 = (f32[1024]{0:T(1024)}, f32[16,32,4]{1,0,2:T(8,128)S(1)}, f32[2,128,4]{1,2,0:T(4,128)}, f32[16]{0:T(128)}, f32[16]{0:T(128)}, /*index=5*/f32[16]{0:T(128)}, f32[16,32]{1,0:T(8,128)}) all-reduce(f32[1024]{0:T(1024)S(1)} %get-tuple-element.74, ...), channel_id=1, replica_groups=mesh['fsdp'=8,'head'=2,'tensor'=2] {'fsdp'}, use_global_device_ids=true, to_apply=%region_21.22 | all-reduce | flops 4656 | bytes 37248 | tf_op jit(solution)/shard_map/psum | solution.py:206
  375.3 4.3 fusion.28
  379.6 8.5 %reduce-scatter.10.cloned.1.call-done = f32[128,256]{1,0:T(8,128)} async-done(((f32[1024,256]{1,0:T(8,128)}), f32[128,256]{1,0:T(8,128)}) %reduce-scatter.10.cloned.1.call-update) | async-done | bytes 131088 | tf_op jit(solution)/shard_map/reduce_scatter | solution.py:196
  389.7 55.8 %reduce-scatter.12.cloned.1.call-done = f32[128,16]{0,1:T(8,128)} async-done(((f32[1024,16]{0,1:T(8,128)}), f32[128,16]{0,1:T(8,128)}) %reduce-scatter.12.cloned.1.call-update) | async-done | bytes 8208 | tf_op jit(solution)/shard_map/reduce_scatter | solution.py:197
  445.5 72.4 %reduce-scatter.14.cloned.1.call-done = f32[16,32,128]{2,1,0:T(8,128)} async-done(((f32[16,32,1024]{2,1,0:T(8,128)}), f32[16,32,128]{2,1,0:T(8,128)}) %reduce-scatter.14.cloned.1.call-update) | async-done | bytes 262160 | tf_op jit(solution)/shard_map/reduce_scatter | solution.py:198
  517.9 72.0 %reduce-scatter.8.cloned.1.call-done = f32[128,16,32]{0,2,1:T(8,128)} async-done(((f32[1024,16,32]{0,2,1:T(8,128)}), f32[128,16,32]{0,2,1:T(8,128)}) %reduce-scatter.8.cloned.1.call-update) | async-done | bytes 262160 | tf_op jit(solution)/shard_map/reduce_scatter | solution.py:190
  590.0 72.1 %reduce-scatter.6.cloned.1.call-done = f32[128,16,32]{0,2,1:T(8,128)} async-done(((f32[1024,16,32]{0,2,1:T(8,128)}), f32[128,16,32]{0,2,1:T(8,128)}) %reduce-scatter.6.cloned.1.call-update) | async-done | bytes 262160 | tf_op jit(solution)/shard_map/reduce_scatter | solution.py:184
  (253 shorter events, 54.8 us)
Async XLA Ops:
  7.2 39.4 %copy-start.69 = (f32[16,32]{1,0:T(8,128)S(1)}, f32[16,32]{1,0:T(8,128)}, u32[]{:S(2)}) copy-start(f32[16,32]{1,0:T(8,128)} %param.26) | copy-start | bytes 6148
  7.2 39.5 %copy-start.70 = (f32[2,128,4]{1,2,0:T(4,128)S(1)}, f32[2,128,4]{1,2,0:T(4,128)}, u32[]{:S(2)}) copy-start(f32[2,128,4]{1,2,0:T(4,128)} %param.22) | copy-start | bytes 12292
  7.2 39.5 %copy-start.75 = (f32[16]{0:T(128)S(1)}, f32[16]{0:T(128)}, u32[]{:S(2)}) copy-start(f32[16]{0:T(128)} %param.25) | copy-start | bytes 196
  7.2 40.2 %copy-start.45 = (f32[16,32,4]{1,2,0:T(4,128)S(1)}, f32[16,32,4]{1,2,0:T(4,128)}, u32[]{:S(2)}) copy-start(f32[16,32,4]{1,2,0:T(4,128)} %param.21) | copy-start | bytes 24580
  7.2 40.9 %copy-start.27 = (bf16[128,2,128]{2,1,0:T(2,128)(2,1)S(1)}, bf16[128,2,128]{2,1,0:T(2,128)(2,1)}, u32[]{:S(2)}) copy-start(bf16[128,2,128]{2,1,0:T(2,128)(2,1)} %param.19) | copy-start | bytes 196612
  7.2 75.6 %all-gather.4.cloned.1.call-start = ((), (), s32[]{:S(2)}) async-start(), calls=%async_computation.5 | async-start | bytes 1179648 | tf_op jit(solution)/shard_map/all_gather | solution.py:91
  8.0 90.6 %all-gather.6.cloned.1.call-start = ((), (), s32[]{:S(2)}) async-start(), calls=%async_computation.6 | async-start | bytes 1179648 | tf_op jit(solution)/shard_map/all_gather | solution.py:92
  8.7 126.8 %all-gather.8.cloned.1.call-start = ((), (), s32[]{:S(2)}) async-start(), calls=%async_computation.7 | async-start | bytes 1179648 | tf_op jit(solution)/shard_map/all_gather | solution.py:95
  9.4 310.1 %all-reduce.28.cloned.1.call-start = ((), (), s32[]{:S(2)}) async-start(), calls=%async_computation.13 | async-start | bytes 9437184 | tf_op jit(solution)/shard_map/psum | solution.py:125
  10.8 70.1 %copy-start = (bf16[512,1024]{1,0:T(8,128)(2,1)S(1)}, bf16[512,1024]{1,0:T(8,128)(2,1)}, u32[]{:S(2)}) copy-start(bf16[512,1024]{1,0:T(8,128)(2,1)} %param.14) | copy-start | bytes 3145732
  10.8 70.1 %copy-start.30 = (f32[1024]{0:T(1024)S(1)}, f32[1024]{0:T(1024)}, u32[]{:S(2)}) copy-start(f32[1024]{0:T(1024)} %param.16) | copy-start | bytes 12292
  13.0 85.6 %copy-start.32 = (f32[512]{0:T(512)}, f32[512]{0:T(512)S(1)}, u32[]{:S(2)}) copy-start(f32[512]{0:T(512)S(1)} %get-tuple-element.141) | copy-start | bytes 6148
  45.0 37.6 %copy-start.34 = (f32[2,16,2]{1,2,0:T(2,128)}, f32[2,16,2]{1,2,0:T(2,128)S(1)}, u32[]{:S(2)}) copy-start(f32[2,16,2]{1,2,0:T(2,128)S(1)} %slice.130) | copy-start | bytes 772
  45.0 44.9 %copy-start.25 = (f32[2,256,16]{1,2,0:T(8,128)}, f32[2,256,16]{1,2,0:T(8,128)S(1)}, u32[]{:S(2)}) copy-start(f32[2,256,16]{1,2,0:T(8,128)S(1)} %bitcast_bitcast_fusion.1) | copy-start | bytes 98308
  45.2 143.0 %copy-start.36 = (f32[2,16]{1,0:T(2,128)}, f32[2,16]{1,0:T(2,128)S(1)}, u32[]{:S(2)}) copy-start(f32[2,16]{1,0:T(2,128)S(1)} %slice_reduce_fusion.2) | copy-start | bytes 388
  46.6 137.8 %copy-start.38 = (f32[512]{0:T(512)}, f32[512]{0:T(512)S(1)}, u32[]{:S(2)}) copy-start(f32[512]{0:T(512)S(1)} %mul.547) | copy-start | bytes 6148
  47.5 37.5 %copy-start.50 = (f32[512,1]{0,1:T(1,128)}, f32[512,1]{0,1:T(1,128)S(1)}, u32[]{:S(2)}) copy-start(f32[512,1]{0,1:T(1,128)S(1)} %get-tuple-element.132) | copy-start | bytes 6148
  47.6 37.5 %copy-start.52 = (f32[512,1]{0,1:T(1,128)}, f32[512,1]{0,1:T(1,128)S(1)}, u32[]{:S(2)}) copy-start(f32[512,1]{0,1:T(1,128)S(1)} %get-tuple-element.133) | copy-start | bytes 6148
  47.6 37.5 %copy-start.54 = (f32[512,1]{0,1:T(1,128)}, f32[512,1]{0,1:T(1,128)S(1)}, u32[]{:S(2)}) copy-start(f32[512,1]{0,1:T(1,128)S(1)} %get-tuple-element.134) | copy-start | bytes 6148
  47.6 37.5 %copy-start.56 = (f32[512,1]{0,1:T(1,128)}, f32[512,1]{0,1:T(1,128)S(1)}, u32[]{:S(2)}) copy-start(f32[512,1]{0,1:T(1,128)S(1)} %get-tuple-element.135) | copy-start | bytes 6148
  110.0 74.5 %copy-start.40 = (f32[512]{0:T(512)}, f32[512]{0:T(512)S(1)}, u32[]{:S(2)}) copy-start(f32[512]{0:T(512)S(1)} %get-tuple-element.143) | copy-start | bytes 6148
  226.8 92.7 %copy-start.13 = (f32[512,256]{1,0:T(8,128)S(1)}, f32[512,256]{1,0:T(8,128)}, u32[]{:S(2)}) copy-start(f32[512,256]{1,0:T(8,128)} %copy-done.12) | copy-start | bytes 1572868
  226.9 94.3 %copy-start.61 = (f32[256,1]{0,1:T(1,128)S(1)}, f32[256,1]{0,1:T(1,128)}, u32[]{:S(2)}) copy-start(f32[256,1]{0,1:T(1,128)} %copy-done.60) | copy-start | bytes 3076
  226.9 94.3 %copy-start.63 = (f32[256,1]{0,1:T(1,128)S(1)}, f32[256,1]{0,1:T(1,128)}, u32[]{:S(2)}) copy-start(f32[256,1]{0,1:T(1,128)} %copy-done.62) | copy-start | bytes 3076
  226.9 94.3 %copy-start.65 = (f32[256,1]{0,1:T(1,128)S(1)}, f32[256,1]{0,1:T(1,128)}, u32[]{:S(2)}) copy-start(f32[256,1]{0,1:T(1,128)} %copy-done.64) | copy-start | bytes 3076
  226.9 94.3 %copy-start.67 = (f32[256,1]{0,1:T(1,128)S(1)}, f32[256,1]{0,1:T(1,128)}, u32[]{:S(2)}) copy-start(f32[256,1]{0,1:T(1,128)} %copy-done.66) | copy-start | bytes 3076
  226.9 161.2 %reduce-scatter.10.cloned.1.call-start = ((), (), s32[]{:S(2)}) async-start(), calls=%async_computation.10 | async-start | bytes 1179648 | tf_op jit(solution)/shard_map/reduce_scatter | solution.py:196
  323.5 122.0 %reduce-scatter.12.cloned.1.call-start = ((), (), s32[]{:S(2)}) async-start(), calls=%async_computation.11 | async-start | bytes 73728 | tf_op jit(solution)/shard_map/reduce_scatter | solution.py:197
  324.6 193.3 %reduce-scatter.14.cloned.1.call-start = ((), (), s32[]{:S(2)}) async-start(), calls=%async_computation.12 | async-start | bytes 2359296 | tf_op jit(solution)/shard_map/reduce_scatter | solution.py:198
  328.1 261.9 %reduce-scatter.8.cloned.1.call-start = ((), (), s32[]{:S(2)}) async-start(), calls=%async_computation.9 | async-start | bytes 2359296 | tf_op jit(solution)/shard_map/reduce_scatter | solution.py:190
  331.4 330.7 %reduce-scatter.6.cloned.1.call-start = ((), (), s32[]{:S(2)}) async-start(), calls=%async_computation.8 | async-start | bytes 2359296 | tf_op jit(solution)/shard_map/reduce_scatter | solution.py:184
  333.8 41.4 %copy-start.68 = (f32[512]{0:T(512)S(1)}, f32[512]{0:T(512)}, u32[]{:S(2)}) copy-start(f32[512]{0:T(512)} %get-tuple-element.140) | copy-start | bytes 6148
  (54 other events, 355.7 us)
Sparse Core Ops, SparseCore 0:
  10.1 43.5 all-gather.3
  55.8 39.1 all-gather.5
  97.1 38.3 all-gather.7
  227.0 92.4 all-reduce.27
  323.6 64.4 reduce-scatter.9
  391.7 53.8 reduce-scatter.11
  449.6 68.2 reduce-scatter.13
  522.0 67.8 reduce-scatter.7
  594.1 67.9 reduce-scatter.5
where the time goes:
time: 679 us; the launch traced here: 669 us
  waiting for transfers between devices  401 us (59%)
  blocking collectives  122 us (18%)
  matrix products  76.5 us (11%)
  other arithmetic  32.2 us (5%)
  local copies, waits for them, and re-layouts  21.5 us (3%)
  between operations  15 us (2%)
    psum x1, waiting for transfers between devices, on_device(): summed = lax.psum(partial_out, ('head', 'tensor'))  92.6 us
    reduce_scatter x1, waiting for transfers between devices, on_device(): lax.psum_scatter(g_w_out.reshape(head_count, head_width, model_width), 'f...  72.4 us
    reduce_scatter x1, waiting for transfers between devices, on_device(): lax.psum_scatter(g_w_x.reshape(model_width, head_count, head_width), 'fsd...  72.1 us
    reduce_scatter x1, waiting for transfers between devices, on_device(): lax.psum_scatter(g_w_z.reshape(model_width, head_count, head_width), 'fsd...  72 us
    reduce_scatter x1, waiting for transfers between devices, on_device(): lax.psum_scatter(g_w_dt, 'fsdp', scatter_dimension=0, tiled=True)  55.8 us
    psum x1, blocking collectives, on_device(): lax.psum((g_norm_gain, g_conv_x.reshape(head_count, head_width, taps), g_...  38.1 us
    all_gather x1, blocking collectives, on_device(): lax.all_gather(weights[2], 'fsdp', axis=0, tiled=True)  32 us
    all_gather x1, blocking collectives, on_device(): lax.all_gather(weights[3], 'fsdp', axis=0, tiled=True)  28.3 us
  transfers between devices with their start and end apart: 9, of which 7 were waited for; matrix products, arithmetic and copies ran while one was open for 7% of the time, Pallas kernels for 0%

commit v1 on v0

--- a/solution.py
+++ b/solution.py
@@ -122,7 +122,9 @@
     scale_out = lax.rsqrt(square_sum / full_inner + EPSILON)[:, None]
     normed_out = (gated * scale_out * gain_flat).astype(jnp.bfloat16)
     partial_out = jnp.dot(normed_out, weight_out, preferred_element_type=jnp.float32)
-    summed = lax.psum(partial_out, ("head", "tensor"))
+    summed = partial_out
+    for axis in ("tensor", "head"):
+        summed = lax.psum(summed, axis)
     block_out = (summed + features).astype(jnp.bfloat16)
     again = (
         lax.all_gather(weights[0], "fsdp", axis=0, tiled=True),

time: 679 us -> 732 us (1.078)
  waiting for transfers between devices: 401 us -> 453 us
    psum x1 -> x3, waiting for transfers between devices: 92.6 us -> 137 us  [the longest x2 82.2 us: on_device(): summed = lax.psum(summed, axis)]
    reduce_scatter x1, waiting for transfers between devices: 8.55 us -> 16.2 us  [on_device(): lax.psum_scatter(g_w_bc, 'fsdp', scatter_dimension=0, tiled=True)]
  transfers between devices with their start and end apart: 9 -> 11, of which waited for: 7 -> 9; matrix products, arithmetic and copies ran while one was open for 7% -> 8% of each run, Pallas kernels for 0% -> 0%
where the time goes in v1:
time: 732 us; the launch traced here: 721 us
  waiting for transfers between devices  453 us (62%)
  blocking collectives  122 us (17%)
  matrix products  77.8 us (11%)
  other arithmetic  32.3 us (4%)
  local copies, waits for them, and re-layouts  21.1 us (3%)
  between operations  15 us (2%)
    psum x2, waiting for transfers between devices, on_device(): summed = lax.psum(summed, axis)  82.2 us
    reduce_scatter x1, waiting for transfers between devices, on_device(): lax.psum_scatter(g_w_x.reshape(model_width, head_count, head_width), 'fsd...  72.3 us
    reduce_scatter x1, waiting for transfers between devices, on_device(): lax.psum_scatter(g_w_out.reshape(head_count, head_width, model_width), 'f...  72.1 us
    reduce_scatter x1, waiting for transfers between devices, on_device(): lax.psum_scatter(g_w_z.reshape(model_width, head_count, head_width), 'fsd...  71.8 us
    reduce_scatter x1, waiting for transfers between devices, on_device(): lax.psum_scatter(g_w_dt, 'fsdp', scatter_dimension=0, tiled=True)  55.4 us
    psum x1, waiting for transfers between devices, on_device(): lax.psum(local_part, ('head', 'tensor'))  54.5 us
    psum x1, blocking collectives, on_device(): lax.psum((g_norm_gain, g_conv_x.reshape(head_count, head_width, taps), g_...  38.5 us
    all_gather x1, blocking collectives, on_device(): lax.all_gather(weights[2], 'fsdp', axis=0, tiled=True)  31.8 us
  transfers between devices with their start and end apart: 11, of which 9 were waited for; matrix products, arithmetic and copies ran while one was open for 8% of the time, Pallas kernels for 0%

profile of v1, /device:TPU:0, one launch (start us, length us, event | category | flops | bytes accessed | tf_op | source)
XLA Modules:
  0.0 721.3 jit_solution(16568742767415864660)
XLA Ops:
  13.0 28.3 %all_gather.22 = bf16[1024,16]{0,1:T(8,128)(2,1)S(1)} all-gather(bf16[128,16]{0,1:T(8,128)(2,1)} %param.20), channel_id=1, replica_groups=mesh['fsdp'=8,'head'=2,'tensor'=2] {'fsdp'}, dimensions={0}, use_global_device_ids=true | all-gather | bytes 36864 | tf_op jit(solution)/shard_map/all_gather | solution.py:94
  48.2 31.8 %all_gather.21 = bf16[1024,2,128]{2,1,0:T(2,128)(2,1)S(1)} all-gather(bf16[128,2,128]{2,1,0:T(2,128)(2,1)S(1)} %copy-done.26), channel_id=1, replica_groups=mesh['fsdp'=8,'head'=2,'tensor'=2] {'fsdp'}, dimensions={0}, use_global_device_ids=true | all-gather | bytes 589824 | tf_op jit(solution)/shard_map/all_gather | solution.py:93
  89.8 6.3 fusion.38
  98.4 3.5 multiply_reduce_fusion.9
  102.0 7.6 %psum.119 = f32[512]{0:T(512)S(1)} all-reduce(f32[512]{0:T(512)S(1)} %get-tuple-element.105), channel_id=1, replica_groups=mesh['fsdp'=8,'head'=2,'tensor'=2] {'head','tensor'}, use_global_device_ids=true, to_apply=%region_4.5 | all-reduce | flops 512 | bytes 4096 | tf_op jit(solution)/shard_map/psum | solution.py:121
  109.6 26.2 %all-gather.8.cloned.1.call-done = bf16[16,32,1024]{2,1,0:T(8,128)(2,1)} async-done(((bf16[16,32,128]{2,1,0:T(8,128)(2,1)}), bf16[16,32,1024]{2,1,0:T(8,128)(2,1)}) %all-gather.8.cloned.1.call-update) | async-done | bytes 1048592 | tf_op jit(solution)/shard_map/all_gather | solution.py:95
  135.8 3.9 multiply_reduce_fusion.3
  139.7 7.5 %psum.122 = f32[512]{0:T(512)S(1)} all-reduce(f32[512]{0:T(512)S(1)} %get-tuple-element.77), channel_id=1, replica_groups=mesh['fsdp'=8,'head'=2,'tensor'=2] {'head','tensor'}, use_global_device_ids=true, to_apply=%region_8.9 | all-reduce | flops 512 | bytes 4096 | tf_op jit(solution)/shard_map/psum | solution.py:146
  147.2 4.3 fusion.45
  152.9 2.9 reshape_reshape.8
  157.7 2.6 convolution_bitcast_fusion.1
  161.2 2.6 convolution_bitcast_fusion.2
  164.4 11.4 %fusion.9 = (f32[2,256,16]{1,2,0:T(8,128)}, f32[2,256,16]{1,2,0:T(8,128)}, f32[2,256,16]{1,2,0:T(8,128)}, f32[2,256,256]{2,1,0:T(8,128)}) fusion(f32[2,256,16]{1,2,0:T(8,128)S(1)} %bitcast.241, f32[2,256,16]{1,2,0:T(8,128)S(1)} %copy-done.25, f32[2,256,256]{2,1,0:T(8,128)S(1)} %copy-done.19, pred[256,256]{1,0:T(8,128)(4,1)S(1)} %copy-done.28, ...), kind=kOutput, calls=%fused_computation.18 | convolution fusion | flops 836608000 | bytes 2850816 | tf_op jit(solution)/shard_map/transpose(jvp(clsh,cshp->clhp))/dot_general | solution.py:45
  175.9 8.0 %fusion.41 = f32[2,256,16,32]{1,3,2,0:T(8,128)} fusion(f32[2,256,16]{1,2,0:T(8,128)S(1)} %bitcast.242, f32[2,256,16]{1,2,0:T(8,128)S(1)} %copy-done.25, f32[2,256,256]{2,1,0:T(8,128)S(1)} %copy-done.19, pred[256,256]{1,0:T(8,128)(4,1)S(1)} %copy-done.28, f32[2,256,16,32]{1,3,2,0:T(8,128)S(1)} %fusion.58, f32[2,16,32,256]{3,0,2,1:T(2,128)S(1)} %bitcast.207, ...), kind=kOutput, calls=%fused_computation.48 | convolution fusion | flops 816316416 | bytes 3833856 | tf_op jit(solution)/shard_map/transpose(jvp(clsh,cshp->clhp))/dot_general | solution.py:45
  194.2 2.6 copy.141
  197.2 5.0 reduce-window.16
  202.7 3.6 fusion.118
  211.9 8.0 %all-reduce.25 = (bf16[512,16]{0,1:T(8,128)(2,1)S(1)}, f32[16]{0:T(128)S(1)}, f32[16]{0:T(128)S(1)}, f32[16]{0:T(128)S(1)}) all-reduce(f32[512,16]{0,1:T(8,128)S(1)} %get-tuple-element.104, f32[16]{0:T(128)S(1)} %get-tuple-element.103, f32[16]{0:T(128)S(1)} %negate_multiply_fusion, ...), channel_id=1, replica_groups=mesh['fsdp'=8,'head'=2,'tensor'=2] {'tensor'}, use_global_device_ids=true, to_apply=%region_16.17 | all-reduce | flops 8240 | bytes 49536 | tf_op jit(solution)/shard_map/psum | solution.py:156
  219.9 4.0 multiply_add_fusion
  224.6 3.3 fusion.93
  228.0 54.5 %all-reduce.34.cloned.1.call-done = (f32[512,1024]{1,0:T(8,128)}, f32[512,256]{1,0:T(8,128)}) async-done(((f32[512,1024]{1,0:T(8,128)}, f32[512,256]{1,0:T(8,128)}), (f32[512,1024]{1,0:T(8,128)}, f32[512,256]{1,0:T(8,128)})) %all-reduce.34.cloned.1.call-update) | async-done | bytes 2621456 | tf_op jit(solution)/shard_map/psum | solution.py:175
  286.5 61.2 %all-reduce.30.cloned.1.call-done = f32[512,1024]{1,0:T(8,128)} async-done(((f32[512,1024]{1,0:T(8,128)}), f32[512,1024]{1,0:T(8,128)}) %all-reduce.30.cloned.1.call-update) | async-done | bytes 2097168 | tf_op jit(solution)/shard_map/psum | solution.py:127
  348.9 3.4 fusion.92
  358.0 2.7 fusion.31
  360.7 38.5 %all-reduce.23 = (f32[1024]{0:T(1024)}, f32[16,32,4]{1,0,2:T(8,128)S(1)}, f32[2,128,4]{1,2,0:T(4,128)}, f32[16]{0:T(128)}, f32[16]{0:T(128)}, /*index=5*/f32[16]{0:T(128)}, f32[16,32]{1,0:T(8,128)}) all-reduce(f32[1024]{0:T(1024)S(1)} %get-tuple-element.74, ...), channel_id=1, replica_groups=mesh['fsdp'=8,'head'=2,'tensor'=2] {'fsdp'}, use_global_device_ids=true, to_apply=%region_22.23 | all-reduce | flops 4656 | bytes 37248 | tf_op jit(solution)/shard_map/psum | solution.py:208
  399.9 16.2 %reduce-scatter.10.cloned.1.call-done = f32[128,256]{1,0:T(8,128)} async-done(((f32[1024,256]{1,0:T(8,128)}), f32[128,256]{1,0:T(8,128)}) %reduce-scatter.10.cloned.1.call-update) | async-done | bytes 131088 | tf_op jit(solution)/shard_map/reduce_scatter | solution.py:198
  417.7 21.0 %all-reduce.32.cloned.1.call-done = f32[512,1024]{1,0:T(8,128)} async-done(((f32[512,1024]{1,0:T(8,128)}), f32[512,1024]{1,0:T(8,128)}) %all-reduce.32.cloned.1.call-update) | async-done | bytes 2097168 | tf_op jit(solution)/shard_map/psum | solution.py:127
  438.6 4.3 fusion.28
  442.9 55.4 %reduce-scatter.12.cloned.1.call-done = f32[128,16]{0,1:T(8,128)} async-done(((f32[1024,16]{0,1:T(8,128)}), f32[128,16]{0,1:T(8,128)}) %reduce-scatter.12.cloned.1.call-update) | async-done | bytes 8208 | tf_op jit(solution)/shard_map/reduce_scatter | solution.py:199
  498.3 72.1 %reduce-scatter.14.cloned.1.call-done = f32[16,32,128]{2,1,0:T(8,128)} async-done(((f32[16,32,1024]{2,1,0:T(8,128)}), f32[16,32,128]{2,1,0:T(8,128)}) %reduce-scatter.14.cloned.1.call-update) | async-done | bytes 262160 | tf_op jit(solution)/shard_map/reduce_scatter | solution.py:200
  570.4 71.8 %reduce-scatter.8.cloned.1.call-done = f32[128,16,32]{0,2,1:T(8,128)} async-done(((f32[1024,16,32]{0,2,1:T(8,128)}), f32[128,16,32]{0,2,1:T(8,128)}) %reduce-scatter.8.cloned.1.call-update) | async-done | bytes 262160 | tf_op jit(solution)/shard_map/reduce_scatter | solution.py:192
  642.2 72.3 %reduce-scatter.6.cloned.1.call-done = f32[128,16,32]{0,2,1:T(8,128)} async-done(((f32[1024,16,32]{0,2,1:T(8,128)}), f32[128,16,32]{0,2,1:T(8,128)}) %reduce-scatter.6.cloned.1.call-update) | async-done | bytes 262160 | tf_op jit(solution)/shard_map/reduce_scatter | solution.py:186
  (259 shorter events, 59.6 us)
Async XLA Ops:
  7.2 39.4 %copy-start.69 = (f32[16,32]{1,0:T(8,128)S(1)}, f32[16,32]{1,0:T(8,128)}, u32[]{:S(2)}) copy-start(f32[16,32]{1,0:T(8,128)} %param.26) | copy-start | bytes 6148
  7.2 39.5 %copy-start.70 = (f32[2,128,4]{1,2,0:T(4,128)S(1)}, f32[2,128,4]{1,2,0:T(4,128)}, u32[]{:S(2)}) copy-start(f32[2,128,4]{1,2,0:T(4,128)} %param.22) | copy-start | bytes 12292
  7.2 39.5 %copy-start.75 = (f32[16]{0:T(128)S(1)}, f32[16]{0:T(128)}, u32[]{:S(2)}) copy-start(f32[16]{0:T(128)} %param.25) | copy-start | bytes 196
  7.2 40.3 %copy-start.44 = (f32[16,32,4]{1,2,0:T(4,128)S(1)}, f32[16,32,4]{1,2,0:T(4,128)}, u32[]{:S(2)}) copy-start(f32[16,32,4]{1,2,0:T(4,128)} %param.21) | copy-start | bytes 24580
  7.2 40.9 %copy-start.26 = (bf16[128,2,128]{2,1,0:T(2,128)(2,1)S(1)}, bf16[128,2,128]{2,1,0:T(2,128)(2,1)}, u32[]{:S(2)}) copy-start(bf16[128,2,128]{2,1,0:T(2,128)(2,1)} %param.19) | copy-start | bytes 196612
  7.2 75.4 %all-gather.4.cloned.1.call-start = ((), (), s32[]{:S(2)}) async-start(), calls=%async_computation.5 | async-start | bytes 1179648 | tf_op jit(solution)/shard_map/all_gather | solution.py:91
  8.0 90.4 %all-gather.6.cloned.1.call-start = ((), (), s32[]{:S(2)}) async-start(), calls=%async_computation.6 | async-start | bytes 1179648 | tf_op jit(solution)/shard_map/all_gather | solution.py:92
  8.7 127.1 %all-gather.8.cloned.1.call-start = ((), (), s32[]{:S(2)}) async-start(), calls=%async_computation.7 | async-start | bytes 1179648 | tf_op jit(solution)/shard_map/all_gather | solution.py:95
  9.4 273.0 %all-reduce.34.cloned.1.call-start = ((), (), s32[]{:S(2)}) async-start(), calls=%async_computation.15 | async-start | bytes 5242880 | tf_op jit(solution)/shard_map/psum | solution.py:175
  10.8 69.9 %copy-start = (bf16[512,1024]{1,0:T(8,128)(2,1)S(1)}, bf16[512,1024]{1,0:T(8,128)(2,1)}, u32[]{:S(2)}) copy-start(bf16[512,1024]{1,0:T(8,128)(2,1)} %param.14) | copy-start | bytes 3145732
  10.8 69.9 %copy-start.29 = (f32[1024]{0:T(1024)S(1)}, f32[1024]{0:T(1024)}, u32[]{:S(2)}) copy-start(f32[1024]{0:T(1024)} %param.16) | copy-start | bytes 12292
  13.0 85.4 %copy-start.31 = (f32[512]{0:T(512)}, f32[512]{0:T(512)S(1)}, u32[]{:S(2)}) copy-start(f32[512]{0:T(512)S(1)} %get-tuple-element.140) | copy-start | bytes 6148
  45.0 37.3 %copy-start.33 = (f32[2,16,2]{1,2,0:T(2,128)}, f32[2,16,2]{1,2,0:T(2,128)S(1)}, u32[]{:S(2)}) copy-start(f32[2,16,2]{1,2,0:T(2,128)S(1)} %slice.130) | copy-start | bytes 772
  45.1 44.7 %copy-start.24 = (f32[2,256,16]{1,2,0:T(8,128)}, f32[2,256,16]{1,2,0:T(8,128)S(1)}, u32[]{:S(2)}) copy-start(f32[2,256,16]{1,2,0:T(8,128)S(1)} %bitcast_bitcast_fusion.1) | copy-start | bytes 98308
  45.3 140.3 %copy-start.35 = (f32[2,16]{1,0:T(2,128)}, f32[2,16]{1,0:T(2,128)S(1)}, u32[]{:S(2)}) copy-start(f32[2,16]{1,0:T(2,128)S(1)} %slice_reduce_fusion.2) | copy-start | bytes 388
  46.7 100.5 %copy-start.37 = (f32[512]{0:T(512)}, f32[512]{0:T(512)S(1)}, u32[]{:S(2)}) copy-start(f32[512]{0:T(512)S(1)} %mul.547) | copy-start | bytes 6148
  47.6 37.3 %copy-start.49 = (f32[512,1]{0,1:T(1,128)}, f32[512,1]{0,1:T(1,128)S(1)}, u32[]{:S(2)}) copy-start(f32[512,1]{0,1:T(1,128)S(1)} %get-tuple-element.131) | copy-start | bytes 6148
  47.6 37.3 %copy-start.51 = (f32[512,1]{0,1:T(1,128)}, f32[512,1]{0,1:T(1,128)S(1)}, u32[]{:S(2)}) copy-start(f32[512,1]{0,1:T(1,128)S(1)} %get-tuple-element.132) | copy-start | bytes 6148
  109.6 37.6 %copy-start.39 = (f32[512]{0:T(512)}, f32[512]{0:T(512)S(1)}, u32[]{:S(2)}) copy-start(f32[512]{0:T(512)S(1)} %get-tuple-element.142) | copy-start | bytes 6148
  224.0 123.7 %all-reduce.30.cloned.1.call-start = ((), (), s32[]{:S(2)}) async-start(), calls=%async_computation.8 | async-start | bytes 4194304 | tf_op jit(solution)/shard_map/psum | solution.py:127
  227.9 54.6 %copy-start.13 = (f32[512,256]{1,0:T(8,128)S(1)}, f32[512,256]{1,0:T(8,128)}, u32[]{:S(2)}) copy-start(f32[512,256]{1,0:T(8,128)} %copy-done.12) | copy-start | bytes 1572868
  227.9 56.2 %copy-start.60 = (f32[256,1]{0,1:T(1,128)S(1)}, f32[256,1]{0,1:T(1,128)}, u32[]{:S(2)}) copy-start(f32[256,1]{0,1:T(1,128)} %copy-done.59) | copy-start | bytes 3076
  227.9 56.2 %copy-start.62 = (f32[256,1]{0,1:T(1,128)S(1)}, f32[256,1]{0,1:T(1,128)}, u32[]{:S(2)}) copy-start(f32[256,1]{0,1:T(1,128)} %copy-done.61) | copy-start | bytes 3076
  227.9 56.2 %copy-start.64 = (f32[256,1]{0,1:T(1,128)S(1)}, f32[256,1]{0,1:T(1,128)}, u32[]{:S(2)}) copy-start(f32[256,1]{0,1:T(1,128)} %copy-done.63) | copy-start | bytes 3076
  227.9 56.2 %copy-start.66 = (f32[256,1]{0,1:T(1,128)S(1)}, f32[256,1]{0,1:T(1,128)}, u32[]{:S(2)}) copy-start(f32[256,1]{0,1:T(1,128)} %copy-done.65) | copy-start | bytes 3076
  228.0 188.1 %reduce-scatter.10.cloned.1.call-start = ((), (), s32[]{:S(2)}) async-start(), calls=%async_computation.12 | async-start | bytes 1179648 | tf_op jit(solution)/shard_map/reduce_scatter | solution.py:198
  286.5 152.2 %all-reduce.32.cloned.1.call-start = ((), (), s32[]{:S(2)}) async-start(), calls=%async_computation.9 | async-start | bytes 4194304 | tf_op jit(solution)/shard_map/psum | solution.py:127
  347.7 150.6 %reduce-scatter.12.cloned.1.call-start = ((), (), s32[]{:S(2)}) async-start(), calls=%async_computation.13 | async-start | bytes 73728 | tf_op jit(solution)/shard_map/reduce_scatter | solution.py:199
  348.8 221.5 %reduce-scatter.14.cloned.1.call-start = ((), (), s32[]{:S(2)}) async-start(), calls=%async_computation.14 | async-start | bytes 2359296 | tf_op jit(solution)/shard_map/reduce_scatter | solution.py:200
  352.3 289.9 %reduce-scatter.8.cloned.1.call-start = ((), (), s32[]{:S(2)}) async-start(), calls=%async_computation.11 | async-start | bytes 2359296 | tf_op jit(solution)/shard_map/reduce_scatter | solution.py:192
  355.5 359.0 %reduce-scatter.6.cloned.1.call-start = ((), (), s32[]{:S(2)}) async-start(), calls=%async_computation.10 | async-start | bytes 2359296 | tf_op jit(solution)/shard_map/reduce_scatter | solution.py:186
  358.0 80.6 %copy-start.67 = (f32[512]{0:T(512)S(1)}, f32[512]{0:T(512)}, u32[]{:S(2)}) copy-start(f32[512]{0:T(512)} %get-tuple-element.139) | copy-start | bytes 6148
  (56 other events, 435.9 us)
Sparse Core Ops, SparseCore 0:
  10.1 43.4 all-gather.3
  55.7 39.5 all-gather.5
  97.3 38.3 all-gather.7
  224.1 58.3 all-reduce.33
  284.6 63.0 all-reduce.29
  351.5 64.4 reduce-scatter.9
  418.4 20.1 all-reduce.31
  442.3 55.9 reduce-scatter.11
  502.4 67.9 reduce-scatter.13
  574.3 67.8 reduce-scatter.7
  646.3 68.1 reduce-scatter.5
